TPU v7x, 128 devices: a whole 4x4x4 slice. The times are simulated.
128 devices in a mesh: obs: 8 (over z_hi, y), unk: 16 (over z_lo, x, core).
Axes of the slice: x: 4, y: 4, z: 4 (z_hi: 2, z_lo: 2; z = z_hi * 2 + z_lo), core: 2. Of those that a mesh axis runs over, the one named last changes fastest.
Arguments:
- design: float32 [8192, 24576], P('obs', 'unk'), may hold values from -0.0625 to 0.0625
- weights: float32 [8192], P('obs'), may hold values from 0.25 to 4
Outputs:
- factor: float32 [24576, 1024], P(('unk', 'obs'))
All inputs are finite; a program needn't handle non-finite values.
Results may differ from a plain program's by a relative error of at most 0.00011.
Values sent between devices are 32-bit elements; how exact they have to be, the bound alone decides.
No kernel may reach another device: no remote copies, remote signals or barrier semaphores. Data moves between devices by JAX's collectives and lax.ppermute only.
A program may use at most 128 MiB of HBM per device.

v0:
```python
import jax
import jax.numpy as jnp
from jax import lax
from jax.sharding import PartitionSpec as P

PANEL = 512
BLOCK = 128


def spread(block, axis, holder):
    block = jnp.where(lax.axis_index(axis) == holder, block, jnp.zeros_like(block))
    return lax.psum(block, axis)


def apply_lower(diag_factor, values):
    return lax.linalg.triangular_solve(
        diag_factor, values, left_side=False, lower=True, transpose_a=True
    )


def left_looking(top_block, owned_rows):
    width = top_block.shape[0]
    factor_top = jnp.zeros_like(top_block)
    factor_rows = jnp.zeros_like(owned_rows)
    for column_block in range(width // BLOCK):
        offset = column_block * BLOCK
        update_top = top_block[:, offset : offset + BLOCK]
        update_rows = owned_rows[:, offset : offset + BLOCK]
        if offset > 0:
            earlier = factor_top[offset : offset + BLOCK, :offset]
            update_top = update_top - jnp.dot(
                factor_top[:, :offset],
                earlier.T,
                precision=lax.Precision.HIGHEST,
                preferred_element_type=jnp.float32,
            )
            update_rows = update_rows - jnp.dot(
                factor_rows[:, :offset],
                earlier.T,
                precision=lax.Precision.HIGHEST,
                preferred_element_type=jnp.float32,
            )
        diag_factor = jnp.linalg.cholesky(update_top[offset : offset + BLOCK])
        below_top = apply_lower(diag_factor, update_top[offset + BLOCK :])
        new_column = jnp.concatenate(
            [jnp.zeros((offset, BLOCK), jnp.float32), diag_factor, below_top], axis=0
        )
        factor_top = factor_top.at[:, offset : offset + BLOCK].set(new_column)
        factor_rows = factor_rows.at[:, offset : offset + BLOCK].set(
            apply_lower(diag_factor, update_rows)
        )
    return factor_rows


def local(design, weights):
    panel_cols = spread(design[:, : 2 * PANEL], "unk", 0)
    weighted = panel_cols * weights[:, None]
    partial_value = lax.dot_general(
        design,
        weighted,
        (((0,), (0,)), ((), ())),
        precision=lax.Precision.HIGHEST,
        preferred_element_type=jnp.float32,
    )
    owned_rows = lax.psum_scatter(partial_value, "obs", scatter_dimension=0, tiled=True)
    gathered = lax.all_gather(owned_rows, "obs", axis=0, tiled=True)
    top_block = spread(gathered[: 2 * PANEL], "unk", 0)
    return left_looking(top_block, owned_rows)


def solution(mesh):
    return jax.shard_map(
        local,
        mesh=mesh,
        in_specs=(P("obs", "unk"), P("obs")),
        out_specs=P(("unk", "obs"), None),
        check_vma=False,
    )
```

profile of v0, /device:TPU:7, one launch (start us, length us, event | category | flops | bytes accessed | tf_op | source)
XLA Modules:
  0.0 775.2 jit_solution(10792649230344124611)
XLA Ops:
  6.5 4.7 slice.463
  11.3 5.3 copy.46
  16.6 2.8 broadcast_select_fusion.1
  19.5 132.4 %all-reduce.5.cloned.1.call-done = f32[1024,1024]{0,1:T(8,128)} async-done(((f32[1024,1024]{0,1:T(8,128)}), f32[1024,1024]{0,1:T(8,128)}) %all-reduce.5.cloned.1.call-update) | async-done | bytes 4194320 | tf_op jit(solution)/shard_map/psum | solution.py:12
  151.9 24.3 %convolution_bitcast_fusion = f32[1536,1024]{0,1:T(8,128)} fusion(f32[1024,1536]{1,0:T(8,128)} %param.35, f32[1024,1024]{0,1:T(8,128)} %all-reduce.5.cloned.1.call-done, f32[1024]{0:T(1024)S(1)} %copy-done.3), kind=kOutput, calls=%fused_computation | convolution fusion | flops 19328401408 | bytes 16781312 | tf_op jit(solution)/shard_map/dot_general | solution.py:58
  176.3 6.5 copy.44
  182.9 98.6 %reduce-scatter.4.cloned.1.call-done = f32[192,1024]{1,0:T(8,128)} async-done(((f32[1536,1024]{1,0:T(8,128)}), f32[192,1024]{1,0:T(8,128)}) %reduce-scatter.4.cloned.1.call-update) | async-done | bytes 786448 | tf_op jit(solution)/shard_map/reduce_scatter | solution.py:65
  281.5 90.1 %all-gather.2.cloned.1.call-done = f32[1536,1024]{1,0:T(8,128)} async-done(((f32[192,1024]{1,0:T(8,128)}), f32[1536,1024]{1,0:T(8,128)}) %all-gather.2.cloned.1.call-update) | async-done | bytes 6291472 | tf_op jit(solution)/shard_map/all_gather | solution.py:66
  371.6 4.7 slice.519
  376.3 5.3 copy.47
  381.7 2.8 broadcast_select_fusion
  385.9 0.7 compare_reduce_fusion.12
  388.5 1.1 compare_reduce_fusion.8
  390.4 122.7 %all-reduce.7.cloned.1.call-done = f32[1024,1024]{0,1:T(8,128)} async-done(((f32[1024,1024]{0,1:T(8,128)}), f32[1024,1024]{0,1:T(8,128)}) %all-reduce.7.cloned.1.call-update) | async-done | bytes 4194320 | tf_op jit(solution)/shard_map/psum | solution.py:12
  513.1 0.8 slice.520
  514.0 0.9 fusion.101
  514.9 11.7 %cholesky.134 = f32[128,128]{1,0:T(8,128)S(1)} custom-call(f32[128,128]{1,0:T(8,128)S(1)} %fusion.101), custom_call_target="Cholesky" | custom-call | tf_op jit(solution)/shard_map/jit(cholesky)/cholesky | solution.py:43
  527.9 9.8 %custom-call.40 = f32[1,128,128]{1,2,0:T(8,128)S(1)} custom-call(f32[1,128,128]{2,1,0:T(8,128)S(1)} %get-tuple-element.199), custom_call_target="InvertDiagBlocksLowerTriangular" | custom-call | tf_op jit(solution)/shard_map/triangular_solve/custom-call.0 | solution.py:16
  537.7 1.0 fusion.37
  538.8 2.1 fusion.48
  541.6 2.5 scatter.54
  545.2 11.9 %cholesky.145 = f32[128,128]{1,0:T(8,128)S(1)} custom-call(f32[128,128]{1,0:T(8,128)S(1)} %fusion.98), custom_call_target="Cholesky" | custom-call | tf_op jit(solution)/shard_map/jit(cholesky)/cholesky | solution.py:43
  558.4 9.8 %custom-call.41 = f32[1,128,128]{1,2,0:T(8,128)S(1)} custom-call(f32[1,128,128]{2,1,0:T(8,128)S(1)} %get-tuple-element.197), custom_call_target="InvertDiagBlocksLowerTriangular" | custom-call | tf_op jit(solution)/shard_map/triangular_solve/custom-call.0 | solution.py:16
  568.2 0.8 fusion.53
  569.1 1.5 fusion.46
  570.6 2.6 convolution_subtract_fusion
  573.4 11.7 %cholesky.156 = f32[128,128]{1,0:T(8,128)S(1)} custom-call(f32[128,128]{1,0:T(8,128)S(1)} %fusion.95), custom_call_target="Cholesky" | custom-call | tf_op jit(solution)/shard_map/jit(cholesky)/cholesky | solution.py:43
  586.4 9.8 %custom-call.42 = f32[1,128,128]{1,2,0:T(8,128)S(1)} custom-call(f32[1,128,128]{2,1,0:T(8,128)S(1)} %get-tuple-element.195), custom_call_target="InvertDiagBlocksLowerTriangular" | custom-call | tf_op jit(solution)/shard_map/triangular_solve/custom-call.0 | solution.py:16
  596.2 0.7 fusion.57
  596.9 1.0 fusion.36
  597.9 1.3 convolution_subtract_fusion.8
  599.2 1.2 fusion.34
  600.4 2.7 fusion.45
  603.1 3.4 fusion.15
  606.6 11.7 %cholesky.167 = f32[128,128]{1,0:T(8,128)S(1)} custom-call(f32[128,128]{1,0:T(8,128)S(1)} %fusion.92), custom_call_target="Cholesky" | custom-call | tf_op jit(solution)/shard_map/jit(cholesky)/cholesky | solution.py:43
  619.7 9.8 %custom-call.43 = f32[1,128,128]{1,2,0:T(8,128)S(1)} custom-call(f32[1,128,128]{2,1,0:T(8,128)S(1)} %get-tuple-element.193), custom_call_target="InvertDiagBlocksLowerTriangular" | custom-call | tf_op jit(solution)/shard_map/triangular_solve/custom-call.0 | solution.py:16
  630.1 1.5 convolution_subtract_fusion.5
  631.6 1.0 fusion.32
  632.6 2.7 fusion.44
  635.3 4.0 fusion.21
  639.5 12.1 %cholesky.178 = f32[128,128]{1,0:T(8,128)S(1)} custom-call(f32[128,128]{1,0:T(8,128)S(1)} %fusion.89), custom_call_target="Cholesky" | custom-call | tf_op jit(solution)/shard_map/jit(cholesky)/cholesky | solution.py:43
  652.9 9.8 %custom-call.44 = f32[1,128,128]{1,2,0:T(8,128)S(1)} custom-call(f32[1,128,128]{2,1,0:T(8,128)S(1)} %get-tuple-element.191), custom_call_target="InvertDiagBlocksLowerTriangular" | custom-call | tf_op jit(solution)/shard_map/triangular_solve/custom-call.0 | solution.py:16
  663.2 1.5 convolution_subtract_fusion.4
  664.7 1.0 fusion.30
  665.7 2.7 fusion.43
  668.3 4.7 fusion.18
  673.2 11.8 %cholesky.189 = f32[128,128]{1,0:T(8,128)S(1)} custom-call(f32[128,128]{1,0:T(8,128)S(1)} %fusion.86), custom_call_target="Cholesky" | custom-call | tf_op jit(solution)/shard_map/jit(cholesky)/cholesky | solution.py:43
  686.4 9.8 %custom-call.45 = f32[1,128,128]{1,2,0:T(8,128)S(1)} custom-call(f32[1,128,128]{2,1,0:T(8,128)S(1)} %get-tuple-element.189), custom_call_target="InvertDiagBlocksLowerTriangular" | custom-call | tf_op jit(solution)/shard_map/triangular_solve/custom-call.0 | solution.py:16
  696.6 1.7 convolution_subtract_fusion.3
  698.2 1.0 fusion.28
  699.2 2.7 fusion.42
  702.0 5.4 fusion.12
  707.5 11.7 %cholesky.200 = f32[128,128]{1,0:T(8,128)S(1)} custom-call(f32[128,128]{1,0:T(8,128)S(1)} %fusion.83), custom_call_target="Cholesky" | custom-call | tf_op jit(solution)/shard_map/jit(cholesky)/cholesky | solution.py:43
  720.6 10.0 %custom-call.46 = f32[1,128,128]{1,2,0:T(8,128)S(1)} custom-call(f32[1,128,128]{2,1,0:T(8,128)S(1)} %get-tuple-element.187), custom_call_target="InvertDiagBlocksLowerTriangular" | custom-call | tf_op jit(solution)/shard_map/triangular_solve/custom-call.0 | solution.py:16
  730.9 1.8 convolution_subtract_fusion.2
  732.7 0.9 fusion.26
  733.7 2.6 fusion.41
  736.3 6.0 fusion.1
  742.4 11.7 %cholesky.211 = f32[128,128]{1,0:T(8,128)S(1)} custom-call(f32[128,128]{1,0:T(8,128)S(1)} %fusion.80), custom_call_target="Cholesky" | custom-call | tf_op jit(solution)/shard_map/jit(cholesky)/cholesky | solution.py:43
  754.2 0.7 compare_reduce_fusion
  754.9 0.7 fusion.76
  755.6 9.8 %custom-call.47 = f32[1,128,128]{1,2,0:T(8,128)S(1)} custom-call(f32[1,128,128]{2,1,0:T(8,128)S(1)} %fusion.76), custom_call_target="InvertDiagBlocksLowerTriangular" | custom-call | tf_op jit(solution)/shard_map/triangular_solve/custom-call.0 | solution.py:16
  765.4 1.9 convolution_subtract_fusion.6
  767.4 1.0 fusion.24
  (94 shorter events, 17.9 us)
Async XLA Ops:
  6.5 145.4 %all-reduce.5.cloned.1.call-start = ((), (), s32[]{:S(2)}) async-start(), calls=%async_computation.1 | async-start | bytes 8388608 | tf_op jit(solution)/shard_map/psum | solution.py:12
  19.4 132.5 %copy-start.3 = (f32[1024]{0:T(1024)S(1)}, f32[1024]{0:T(1024)}, u32[]{:S(2)}) copy-start(f32[1024]{0:T(1024)} %param.36) | copy-start | bytes 12292
  19.4 262.0 %reduce-scatter.4.cloned.1.call-start = ((), (), s32[]{:S(2)}) async-start(), calls=%async_computation.4 | async-start | bytes 7077888 | tf_op jit(solution)/shard_map/reduce_scatter | solution.py:65
  182.8 188.8 %all-gather.2.cloned.1.call-start = ((), (), s32[]{:S(2)}) async-start(), calls=%async_computation.2 | async-start | bytes 7077888 | tf_op jit(solution)/shard_map/all_gather | solution.py:66
  281.5 231.6 %all-reduce.7.cloned.1.call-start = ((), (), s32[]{:S(2)}) async-start(), calls=%async_computation.3 | async-start | bytes 8388608 | tf_op jit(solution)/shard_map/psum | solution.py:12
  384.5 5.1 copy-start.2
  537.7 6.7 copy-start.1
  730.9 11.4 %slice-start = ((f32[1024,1024]{0,1:T(8,128)}), f32[1024,128]{0,1:T(8,128)S(1)}, s32[]{:S(2)}) async-start(f32[1024,1024]{0,1:T(8,128)} %all-reduce.7.cloned.1.call-done), calls=%async_computation.5 | async-start | bytes 1048576 | tf_op jit(solution)/shard_map/slice | solution.py:27
  733.6 33.7 %copy-start = (f32[192,1024]{1,0:T(8,128)}, f32[192,1024]{1,0:T(8,128)S(1)}, u32[]{:S(2)}) copy-start(f32[192,1024]{1,0:T(8,128)S(1)} %fusion.26) | copy-start | bytes 2359300
Sparse Core Ops, SparseCore 0:
  19.5 132.3 all-reduce.4
  182.9 98.4 reduce-scatter.3
  283.7 87.8 all-gather.1
  384.6 128.3 all-reduce.6
where the time goes:
time: 783 us; the launch traced here: 775 us
  waiting for transfers between devices  444 us (57%)
  other arithmetic  211 us (27%)
  matrix products  74.5 us (10%)
  local copies, waits for them, and re-layouts  31.6 us (4%)
  between operations  14.1 us (2%)
    psum x2, waiting for transfers between devices, spread(): return lax.psum(block, axis)  255 us
    another operation x24, other arithmetic, left_looking(): diag_factor = jnp.linalg.cholesky(update_top[offset:offset + BLOCK])  99.8 us
    reduce_scatter x1, waiting for transfers between devices, local(): lax.psum_scatter(partial_value, 'obs', scatter_dimension=0, tiled=True)  98.6 us
    all_gather x1, waiting for transfers between devices, local(): gathered = lax.all_gather(owned_rows, 'obs', axis=0, tiled=True)  90.1 us
    another operation x16, other arithmetic, apply_lower(): lax.linalg.triangular_solve(diag_factor, values, left_side=False, lower=T...  84 us
    dot_general x7, matrix products, left_looking(): jnp.dot(factor_top[:, :offset], earlier.T, precision=lax.Precision.HIGHES...  26.8 us
    dot_general x1, matrix products, local(): lax.dot_general(design, weighted, (((0,), (0,)), ((), ())), precision=lax...  24.3 us
    unnamed x18, local copies, waits for them, and re-layouts  17.9 us
  transfers between devices with their start and end apart: 4, of which 4 were waited for; matrix products, arithmetic and copies ran while one was open for 1% of the time, Pallas kernels for 0%

commit v1 on v0

--- a/solution.py
+++ b/solution.py
@@ -63,7 +63,15 @@
         preferred_element_type=jnp.float32,
     )
     owned_rows = lax.psum_scatter(partial_value, "obs", scatter_dimension=0, tiled=True)
-    gathered = lax.all_gather(owned_rows, "obs", axis=0, tiled=True)
+    gathered = jnp.concatenate(
+        lax.all_to_all(
+            jnp.stack([owned_rows for _ in range(lax.axis_size("obs"))]),
+            axis_name="obs",
+            split_axis=0,
+            concat_axis=0,
+        ),
+        axis=0,
+    )
     top_block = spread(gathered[: 2 * PANEL], "unk", 0)
     return left_looking(top_block, owned_rows)
 

time: 783 us -> 767 us (0.980)
  waiting for transfers between devices: 444 us -> 357 us
  blocking collectives: 0 us -> 73.6 us
    all_gather x1 -> x0, waiting for transfers between devices: 90.1 us -> none  [local(): gathered = lax.all_gather(owned_rows, 'obs', axis=0, tiled=True)]
    all_to_all x0 -> x1, blocking collectives: none -> 73.6 us  [local(): lax.all_to_all(jnp.stack([owned_rows for _ in range(lax.axis_size('obs'))...]
    unnamed x18 -> x11, local copies, waits for them, and re-layouts: 17.9 us -> 17.2 us
  transfers between devices with their start and end apart: 4 -> 3, of which waited for: 4 -> 3; matrix products, arithmetic and copies ran while one was open for 1% -> 1% of each run, Pallas kernels for 0% -> 0%
where the time goes in v1:
time: 767 us; the launch traced here: 759 us
  waiting for transfers between devices  357 us (47%)
  other arithmetic  211 us (28%)
  blocking collectives  73.6 us (10%)
  matrix products  73.2 us (10%)
  local copies, waits for them, and re-layouts  30.4 us (4%)
  between operations  14 us (2%)
    psum x2, waiting for transfers between devices, spread(): return lax.psum(block, axis)  258 us
    another operation x24, other arithmetic, left_looking(): diag_factor = jnp.linalg.cholesky(update_top[offset:offset + BLOCK])  99.7 us
    reduce_scatter x1, waiting for transfers between devices, local(): lax.psum_scatter(partial_value, 'obs', scatter_dimension=0, tiled=True)  98.6 us
    another operation x16, other arithmetic, apply_lower(): lax.linalg.triangular_solve(diag_factor, values, left_side=False, lower=T...  83.9 us
    all_to_all x1, blocking collectives, local(): lax.all_to_all(jnp.stack([owned_rows for _ in range(lax.axis_size('obs'))...  73.6 us
    dot_general x7, matrix products, left_looking(): jnp.dot(factor_top[:, :offset], earlier.T, precision=lax.Precision.HIGHES...  27.1 us
    dot_general x1, matrix products, local(): lax.dot_general(design, weighted, (((0,), (0,)), ((), ())), precision=lax...  24.3 us
    unnamed x11, local copies, waits for them, and re-layouts  17.2 us
  transfers between devices with their start and end apart: 3, of which 3 were waited for; matrix products, arithmetic and copies ran while one was open for 1% of the time, Pallas kernels for 0%

profile of v1, /device:TPU:7, one launch (start us, length us, event | category | flops | bytes accessed | tf_op | source)
XLA Modules:
  0.0 758.7 jit_solution(7355347581811947366)
XLA Ops:
  6.5 4.7 slice.463
  11.3 5.3 copy.71
  16.6 2.8 broadcast_select_fusion.1
  19.5 132.4 %all-reduce.5.cloned.1.call-done = f32[1024,1024]{0,1:T(8,128)} async-done(((f32[1024,1024]{0,1:T(8,128)}), f32[1024,1024]{0,1:T(8,128)}) %all-reduce.5.cloned.1.call-update) | async-done | bytes 4194320 | tf_op jit(solution)/shard_map/psum | solution.py:12
  151.9 24.3 %convolution_bitcast_fusion = f32[1536,1024]{0,1:T(8,128)} fusion(f32[1024,1536]{1,0:T(8,128)} %param.35, f32[1024,1024]{0,1:T(8,128)} %all-reduce.5.cloned.1.call-done, f32[1024]{0:T(1024)S(1)} %copy-done.3), kind=kOutput, calls=%fused_computation | convolution fusion | flops 19328401408 | bytes 16781312 | tf_op jit(solution)/shard_map/dot_general | solution.py:58
  176.3 6.5 copy.69
  182.9 98.6 %reduce-scatter.4.cloned.1.call-done = f32[192,1024]{1,0:T(8,128)} async-done(((f32[1536,1024]{1,0:T(8,128)}), f32[192,1024]{1,0:T(8,128)}) %reduce-scatter.4.cloned.1.call-update) | async-done | bytes 786448 | tf_op jit(solution)/shard_map/reduce_scatter | solution.py:65
  281.4 1.9 stack.2
  283.3 73.6 %all_to_all.5 = f32[8,192,1024]{2,1,0:T(8,128)S(1)} all-to-all(f32[8,192,1024]{2,1,0:T(8,128)S(1)} %stack.2), channel_id=1, replica_groups=mesh['obs'=8,'unk'=16] {'obs'}, dimensions={0} | all-to-all | bytes 12582912 | tf_op jit(solution)/shard_map/all_to_all | solution.py:67
  356.9 2.2 slice.519
  359.1 5.3 copy.72
  364.5 2.8 broadcast_select_fusion
  371.2 1.1 compare_reduce_fusion.8
  372.3 125.9 %all-reduce.7.cloned.1.call-done = f32[1024,1024]{0,1:T(8,128)} async-done(((f32[1024,1024]{0,1:T(8,128)}), f32[1024,1024]{0,1:T(8,128)}) %all-reduce.7.cloned.1.call-update) | async-done | bytes 4194320 | tf_op jit(solution)/shard_map/psum | solution.py:12
  498.2 0.8 slice.520
  499.1 0.9 fusion.101
  500.0 11.7 %cholesky.134 = f32[128,128]{1,0:T(8,128)S(1)} custom-call(f32[128,128]{1,0:T(8,128)S(1)} %fusion.101), custom_call_target="Cholesky" | custom-call | tf_op jit(solution)/shard_map/jit(cholesky)/cholesky | solution.py:43
  513.1 9.8 %custom-call.40 = f32[1,128,128]{1,2,0:T(8,128)S(1)} custom-call(f32[1,128,128]{2,1,0:T(8,128)S(1)} %get-tuple-element.199), custom_call_target="InvertDiagBlocksLowerTriangular" | custom-call | tf_op jit(solution)/shard_map/triangular_solve/custom-call.0 | solution.py:16
  522.9 1.0 fusion.37
  524.0 2.1 fusion.48
  526.7 2.5 scatter.54
  530.0 11.7 %cholesky.145 = f32[128,128]{1,0:T(8,128)S(1)} custom-call(f32[128,128]{1,0:T(8,128)S(1)} %fusion.98), custom_call_target="Cholesky" | custom-call | tf_op jit(solution)/shard_map/jit(cholesky)/cholesky | solution.py:43
  541.8 0.8 compare_reduce_fusion.6
  543.2 9.8 %custom-call.41 = f32[1,128,128]{1,2,0:T(8,128)S(1)} custom-call(f32[1,128,128]{2,1,0:T(8,128)S(1)} %get-tuple-element.197), custom_call_target="InvertDiagBlocksLowerTriangular" | custom-call | tf_op jit(solution)/shard_map/triangular_solve/custom-call.0 | solution.py:16
  553.0 0.8 fusion.53
  553.9 1.5 fusion.46
  555.4 2.6 convolution_subtract_fusion
  558.2 11.7 %cholesky.156 = f32[128,128]{1,0:T(8,128)S(1)} custom-call(f32[128,128]{1,0:T(8,128)S(1)} %fusion.95), custom_call_target="Cholesky" | custom-call | tf_op jit(solution)/shard_map/jit(cholesky)/cholesky | solution.py:43
  571.2 9.8 %custom-call.42 = f32[1,128,128]{1,2,0:T(8,128)S(1)} custom-call(f32[1,128,128]{2,1,0:T(8,128)S(1)} %get-tuple-element.195), custom_call_target="InvertDiagBlocksLowerTriangular" | custom-call | tf_op jit(solution)/shard_map/triangular_solve/custom-call.0 | solution.py:16
  582.0 0.9 fusion.36
  582.9 1.2 convolution_subtract_fusion.8
  584.1 0.8 fusion.34
  584.9 2.6 fusion.45
  587.5 3.6 fusion.15
  591.3 11.7 %cholesky.167 = f32[128,128]{1,0:T(8,128)S(1)} custom-call(f32[128,128]{1,0:T(8,128)S(1)} %fusion.92), custom_call_target="Cholesky" | custom-call | tf_op jit(solution)/shard_map/jit(cholesky)/cholesky | solution.py:43
  604.3 9.8 %custom-call.43 = f32[1,128,128]{1,2,0:T(8,128)S(1)} custom-call(f32[1,128,128]{2,1,0:T(8,128)S(1)} %get-tuple-element.193), custom_call_target="InvertDiagBlocksLowerTriangular" | custom-call | tf_op jit(solution)/shard_map/triangular_solve/custom-call.0 | solution.py:16
  614.7 1.4 convolution_subtract_fusion.7
  616.1 0.9 fusion.32
  617.0 2.7 fusion.44
  619.7 4.0 fusion.21
  623.9 12.1 %cholesky.178 = f32[128,128]{1,0:T(8,128)S(1)} custom-call(f32[128,128]{1,0:T(8,128)S(1)} %fusion.89), custom_call_target="Cholesky" | custom-call | tf_op jit(solution)/shard_map/jit(cholesky)/cholesky | solution.py:43
  637.3 9.8 %custom-call.44 = f32[1,128,128]{1,2,0:T(8,128)S(1)} custom-call(f32[1,128,128]{2,1,0:T(8,128)S(1)} %get-tuple-element.191), custom_call_target="InvertDiagBlocksLowerTriangular" | custom-call | tf_op jit(solution)/shard_map/triangular_solve/custom-call.0 | solution.py:16
  647.6 1.4 convolution_subtract_fusion.5
  649.1 0.8 fusion.30
  649.9 2.7 fusion.43
  652.6 4.7 fusion.18
  657.5 11.7 %cholesky.189 = f32[128,128]{1,0:T(8,128)S(1)} custom-call(f32[128,128]{1,0:T(8,128)S(1)} %fusion.86), custom_call_target="Cholesky" | custom-call | tf_op jit(solution)/shard_map/jit(cholesky)/cholesky | solution.py:43
  670.5 9.9 %custom-call.45 = f32[1,128,128]{1,2,0:T(8,128)S(1)} custom-call(f32[1,128,128]{2,1,0:T(8,128)S(1)} %get-tuple-element.189), custom_call_target="InvertDiagBlocksLowerTriangular" | custom-call | tf_op jit(solution)/shard_map/triangular_solve/custom-call.0 | solution.py:16
  680.8 1.6 convolution_subtract_fusion.4
  682.4 0.9 fusion.28
  683.3 2.7 fusion.42
  686.0 5.4 fusion.12
  691.6 11.7 %cholesky.200 = f32[128,128]{1,0:T(8,128)S(1)} custom-call(f32[128,128]{1,0:T(8,128)S(1)} %fusion.83), custom_call_target="Cholesky" | custom-call | tf_op jit(solution)/shard_map/jit(cholesky)/cholesky | solution.py:43
  704.7 9.8 %custom-call.46 = f32[1,128,128]{1,2,0:T(8,128)S(1)} custom-call(f32[1,128,128]{2,1,0:T(8,128)S(1)} %get-tuple-element.187), custom_call_target="InvertDiagBlocksLowerTriangular" | custom-call | tf_op jit(solution)/shard_map/triangular_solve/custom-call.0 | solution.py:16
  714.8 1.9 convolution_subtract_fusion.3
  716.7 0.8 fusion.26
  717.5 2.6 fusion.41
  720.2 6.0 fusion.1
  726.3 11.7 %cholesky.211 = f32[128,128]{1,0:T(8,128)S(1)} custom-call(f32[128,128]{1,0:T(8,128)S(1)} %fusion.80), custom_call_target="Cholesky" | custom-call | tf_op jit(solution)/shard_map/jit(cholesky)/cholesky | solution.py:43
  738.1 0.7 compare_reduce_fusion
  738.8 0.7 fusion.76
  739.5 9.8 %custom-call.47 = f32[1,128,128]{1,2,0:T(8,128)S(1)} custom-call(f32[1,128,128]{2,1,0:T(8,128)S(1)} %fusion.76), custom_call_target="InvertDiagBlocksLowerTriangular" | custom-call | tf_op jit(solution)/shard_map/triangular_solve/custom-call.0 | solution.py:16
  749.3 1.8 convolution_subtract_fusion.2
  751.1 0.9 fusion.24
  (85 shorter events, 17.8 us)
Async XLA Ops:
  6.5 145.4 %all-reduce.5.cloned.1.call-start = ((), (), s32[]{:S(2)}) async-start(), calls=%async_computation.2 | async-start | bytes 8388608 | tf_op jit(solution)/shard_map/psum | solution.py:12
  19.4 132.5 %copy-start.3 = (f32[1024]{0:T(1024)S(1)}, f32[1024]{0:T(1024)}, u32[]{:S(2)}) copy-start(f32[1024]{0:T(1024)} %param.36) | copy-start | bytes 12292
  19.4 262.0 %reduce-scatter.4.cloned.1.call-start = ((), (), s32[]{:S(2)}) async-start(), calls=%async_computation.4 | async-start | bytes 7077888 | tf_op jit(solution)/shard_map/reduce_scatter | solution.py:65
  182.8 315.4 %all-reduce.7.cloned.1.call-start = ((), (), s32[]{:S(2)}) async-start(), calls=%async_computation.3 | async-start | bytes 8388608 | tf_op jit(solution)/shard_map/psum | solution.py:12
  367.3 155.6 %copy-start.2 = (f32[192,1024]{1,0:T(8,128)S(1)}, f32[192,1024]{1,0:T(8,128)}, u32[]{:S(2)}) copy-start(f32[192,1024]{1,0:T(8,128)} %reduce-scatter.4.cloned.1.call-done) | copy-start | bytes 2359300
  522.9 6.3 copy-start.1
  714.8 11.4 %slice-start = ((f32[1024,1024]{0,1:T(8,128)}), f32[1024,128]{0,1:T(8,128)S(1)}, s32[]{:S(2)}) async-start(f32[1024,1024]{0,1:T(8,128)} %all-reduce.7.cloned.1.call-done), calls=%async_computation.5 | async-start | bytes 1048576 | tf_op jit(solution)/shard_map/slice | solution.py:27
  717.5 33.6 %copy-start = (f32[192,1024]{1,0:T(8,128)}, f32[192,1024]{1,0:T(8,128)S(1)}, u32[]{:S(2)}) copy-start(f32[192,1024]{1,0:T(8,128)S(1)} %fusion.26) | copy-start | bytes 2359300
Sparse Core Ops, SparseCore 0:
  19.5 132.3 all-reduce.4
  182.9 98.4 reduce-scatter.3
  367.4 130.7 all-reduce.6
